TPU v7x, 512 devices: a whole 4x4x16 slice. The times are simulated.
512 devices in a mesh: mem: 32 (over z, core), space: 16 (over y, x).
Axes of the slice: x: 4, y: 4, z: 16, core: 2. Of those that a mesh axis runs over, the one named last changes fastest.
Arguments:
- ensemble: bfloat16 [1024, 262144], P('mem', 'space'), may hold values from -420 to 420, as said below
- log_weights: float32 [1024], replicated, may hold values from -405 to -195, as said below
Outputs:
- analysis: bfloat16 [1024, 262144], P('mem', 'space')
Inputs may be any that keep to these rules, and one draw needn't show every extreme that they name: `ensemble`: finite values. `log_weights`: unnormalized log-likelihoods; only differences between members matter.
All inputs are finite; a program needn't handle non-finite values.
Results may differ from a plain program's by a relative error of at most 0.003.
The roundings to bfloat16 on the way count: a program that leaves them out, or rounds other values in their place, can miss the bound.
Values may be sent and summed in bfloat16 or wider, within the bound.
No kernel may reach another device: no remote copies, remote signals or barrier semaphores. Data moves between devices by JAX's collectives and lax.ppermute only.
A program may use at most 64 MiB of HBM per device.

v0:
```python
import jax
import jax.numpy as jnp
from jax import lax
from jax.sharding import PartitionSpec as P

M = 1024
ITERS = 10


def coupling_from(kernel_part, weights_part, total_sum):

    def sweep(step, carry):
        row_scale, col_scale = carry
        row_scale = weights_part / jnp.dot(kernel_part, col_scale, precision=lax.Precision.HIGHEST)
        sums = total_sum(jnp.dot(row_scale, kernel_part, precision=lax.Precision.HIGHEST))
        return (row_scale, 1.0 / M / sums)

    start_col = jnp.ones((kernel_part.shape[1],), jnp.float32)
    row_scale, col_scale = lax.fori_loop(0, ITERS, sweep, (weights_part, start_col))
    return (M * row_scale[:, None] * kernel_part * col_scale[None, :]).astype(jnp.bfloat16)


def per_device(ensemble, log_weights):
    members_dev = ensemble.shape[0]
    cells_total = ensemble.shape[1] * lax.axis_size("space")
    relaid = lax.all_to_all(ensemble, "mem", split_axis=1, concat_axis=0, tiled=True)
    partial_gram = lax.dot_general(
        relaid, relaid, (((1,), (1,)), ((), ())), preferred_element_type=jnp.float32
    )
    weights = jax.nn.softmax(log_weights)
    local_rows = lax.psum_scatter(partial_gram, "mem", scatter_dimension=0, tiled=True)
    gram_rows = lax.psum(local_rows, "space")
    start = lax.axis_index("mem") * members_dev
    own_block = lax.dynamic_slice_in_dim(gram_rows, start, members_dev, 1)
    own_norms = jnp.sum(own_block * jnp.eye(members_dev, dtype=jnp.float32), axis=1)
    all_norms = lax.all_gather(own_norms, "mem", axis=0, tiled=True)
    dist = (own_norms[:, None] + all_norms[None, :] - 2.0 * gram_rows) / cells_total
    dist_total = lax.psum(jnp.sum(dist), "mem")
    mean_dist = dist_total / (M * (M - 1))
    kernel = jnp.exp(-dist / (0.08 * mean_dist))
    weights_rows = lax.dynamic_slice_in_dim(weights, start, members_dev, 0)

    def column_total(values):
        return lax.psum(values, "mem")

    coupling_rows = coupling_from(kernel, weights_rows, column_total)
    coupling = lax.all_gather(coupling_rows, "mem", axis=0, tiled=True)
    mixed = lax.dot_general(
        coupling, relaid, (((0,), (0,)), ((), ())), preferred_element_type=jnp.float32
    )
    mixed = mixed.astype(jnp.bfloat16)
    return lax.all_to_all(mixed, "mem", split_axis=0, concat_axis=1, tiled=True)


def solution(mesh):
    return jax.shard_map(
        per_device,
        mesh=mesh,
        in_specs=(P("mem", "space"), P()),
        out_specs=P("mem", "space"),
        check_vma=False,
    )
```

profile of v0, /device:TPU:1, one launch (start us, length us, event | category | flops | bytes accessed | tf_op | source)
XLA Modules:
  0.0 1010.4 jit_solution(11346003454657286297)
XLA Ops:
  6.5 0.0 reduce-scatter.2.cloned.1.call-start
  6.5 1.4 copy.12
  7.9 72.3 %all_to_all.38 = bf16[32,32,512]{2,0,1:T(8,128)(2,1)S(1)} all-to-all(bf16[32,32,512]{2,0,1:T(8,128)(2,1)S(1)} %bitcast.43), channel_id=1, replica_groups=mesh['mem'=32,'space'=16] {'mem'}, dimensions={1} | all-to-all | bytes 2097152 | tf_op jit(solution)/shard_map/all_to_all | solution.py:26
  80.2 3.2 fusion.6
  83.4 0.0 reduce-scatter.2.cloned.1.call-update
  83.4 0.0 all-reduce.3.cloned.1.call-start
  83.5 1.3 dynamic-slice
  85.3 0.0 copy-done.1
  85.3 0.6 reduce_max.9
  85.9 1.2 fusion.5
  87.2 98.8 %reduce-scatter.2.cloned.1.call-done = f32[32,1024]{1,0:T(8,128)} async-done(((f32[1024,1024]{1,0:T(8,128)}), f32[32,1024]{1,0:T(8,128)}) %reduce-scatter.2.cloned.1.call-update) | async-done | bytes 131088 | tf_op jit(solution)/shard_map/reduce_scatter | solution.py:31
  186.0 0.0 all-reduce.3.cloned.1.call-update
  186.0 0.0 all-gather.2.cloned.1.call-start
  186.1 1.2 fusion.4
  187.3 0.1 dynamic_slice.6
  187.4 114.0 %all-reduce.3.cloned.1.call-done = f32[32,1024]{1,0:T(8,128)} async-done(((f32[32,1024]{1,0:T(8,128)}), f32[32,1024]{1,0:T(8,128)}) %all-reduce.3.cloned.1.call-update) | async-done | bytes 131088 | tf_op jit(solution)/shard_map/psum | solution.py:32
  301.4 1.0 select_reduce_fusion
  302.4 0.2 dynamic-update-slice
  302.7 48.6 %all-reduce = f32[1024]{0:T(1024)S(1)} all-reduce(f32[1024]{0:T(1024)S(1)} %dynamic-update-slice), channel_id=1, replica_groups=mesh['mem'=32,'space'=16] {'mem'}, use_global_device_ids=true, to_apply=%add | all-reduce | flops 1024 | bytes 8192
  351.2 1.7 fusion.3
  352.9 0.5 copy.16
  353.4 47.1 %psum.22 = f32[]{:T(128)} all-reduce(f32[]{:T(128)} %fusion.3), channel_id=1, replica_groups=mesh['mem'=32,'space'=16] {'mem'}, use_global_device_ids=true, to_apply=%region_6.0 | all-reduce | flops 1 | bytes 8 | tf_op jit(solution)/shard_map/psum | solution.py:38
  401.2 1.0 divide_exponential_fusion
  402.2 462.6 %while.13 = (s32[]{:T(128)}, f32[32]{0:T(128)}, f32[1024]{0:T(1024)S(1)}, f32[32,1024]{1,0:T(8,128)S(1)}, f32[32]{0:T(128)S(1)}, /*index=5*/s32[]{:T(128)}, s32[]{:T(128)}) while((s32[]{:T(128)}, f32[32]{0:T(128)}, f32[1024]{0:T(1024)S(1)}, f32[32,1024]{1,0:T(8,128)S(1)}, f32[32]{0:T(128)S(1)}, /*index=5*/s32[]{:T(128)}, ...), condition=%wide.region_9.0_spmd.clone, body=%wide.region_7.0_spmd.clone.sunk | while | flops 789539 | bytes 295923 | solution.py:19
  402.2 0.2 fusion.24
  402.4 0.2 fusion.25
  402.6 45.8 %psum.25 = f32[1024]{0:T(1024)S(1)} all-reduce(f32[1024]{0:T(1024)S(1)} %bitcast.49), channel_id=1, replica_groups=mesh['mem'=32,'space'=16] {'mem'}, use_global_device_ids=true, to_apply=%region_8.0 | all-reduce | flops 1024 | bytes 8192 | tf_op jit(solution)/shard_map/while/body/eval_jaxpr/psum | solution.py:44
  448.4 0.0 copy-done.2
  448.5 0.2 fusion.24
  448.7 0.2 fusion.25
  448.9 45.8 %psum.25 = f32[1024]{0:T(1024)S(1)} all-reduce(f32[1024]{0:T(1024)S(1)} %bitcast.49), channel_id=1, replica_groups=mesh['mem'=32,'space'=16] {'mem'}, use_global_device_ids=true, to_apply=%region_8.0 | all-reduce | flops 1024 | bytes 8192 | tf_op jit(solution)/shard_map/while/body/eval_jaxpr/psum | solution.py:44
  494.7 0.0 copy-done.2
  494.7 0.2 fusion.24
  494.9 0.2 fusion.25
  495.2 45.8 %psum.25 = f32[1024]{0:T(1024)S(1)} all-reduce(f32[1024]{0:T(1024)S(1)} %bitcast.49), channel_id=1, replica_groups=mesh['mem'=32,'space'=16] {'mem'}, use_global_device_ids=true, to_apply=%region_8.0 | all-reduce | flops 1024 | bytes 8192 | tf_op jit(solution)/shard_map/while/body/eval_jaxpr/psum | solution.py:44
  541.0 0.2 fusion.24
  541.2 0.2 fusion.25
  541.4 45.8 %psum.25 = f32[1024]{0:T(1024)S(1)} all-reduce(f32[1024]{0:T(1024)S(1)} %bitcast.49), channel_id=1, replica_groups=mesh['mem'=32,'space'=16] {'mem'}, use_global_device_ids=true, to_apply=%region_8.0 | all-reduce | flops 1024 | bytes 8192 | tf_op jit(solution)/shard_map/while/body/eval_jaxpr/psum | solution.py:44
  587.3 0.2 fusion.24
  587.4 0.2 fusion.25
  587.7 45.8 %psum.25 = f32[1024]{0:T(1024)S(1)} all-reduce(f32[1024]{0:T(1024)S(1)} %bitcast.49), channel_id=1, replica_groups=mesh['mem'=32,'space'=16] {'mem'}, use_global_device_ids=true, to_apply=%region_8.0 | all-reduce | flops 1024 | bytes 8192 | tf_op jit(solution)/shard_map/while/body/eval_jaxpr/psum | solution.py:44
  633.5 0.2 fusion.24
  633.7 0.2 fusion.25
  633.9 45.8 %psum.25 = f32[1024]{0:T(1024)S(1)} all-reduce(f32[1024]{0:T(1024)S(1)} %bitcast.49), channel_id=1, replica_groups=mesh['mem'=32,'space'=16] {'mem'}, use_global_device_ids=true, to_apply=%region_8.0 | all-reduce | flops 1024 | bytes 8192 | tf_op jit(solution)/shard_map/while/body/eval_jaxpr/psum | solution.py:44
  679.8 0.2 fusion.24
  680.0 0.2 fusion.25
  680.2 45.8 %psum.25 = f32[1024]{0:T(1024)S(1)} all-reduce(f32[1024]{0:T(1024)S(1)} %bitcast.49), channel_id=1, replica_groups=mesh['mem'=32,'space'=16] {'mem'}, use_global_device_ids=true, to_apply=%region_8.0 | all-reduce | flops 1024 | bytes 8192 | tf_op jit(solution)/shard_map/while/body/eval_jaxpr/psum | solution.py:44
  726.0 0.2 fusion.24
  726.2 0.2 fusion.25
  726.5 45.8 %psum.25 = f32[1024]{0:T(1024)S(1)} all-reduce(f32[1024]{0:T(1024)S(1)} %bitcast.49), channel_id=1, replica_groups=mesh['mem'=32,'space'=16] {'mem'}, use_global_device_ids=true, to_apply=%region_8.0 | all-reduce | flops 1024 | bytes 8192 | tf_op jit(solution)/shard_map/while/body/eval_jaxpr/psum | solution.py:44
  772.3 0.2 fusion.24
  772.5 0.2 fusion.25
  772.7 45.8 %psum.25 = f32[1024]{0:T(1024)S(1)} all-reduce(f32[1024]{0:T(1024)S(1)} %bitcast.49), channel_id=1, replica_groups=mesh['mem'=32,'space'=16] {'mem'}, use_global_device_ids=true, to_apply=%region_8.0 | all-reduce | flops 1024 | bytes 8192 | tf_op jit(solution)/shard_map/while/body/eval_jaxpr/psum | solution.py:44
  818.6 0.2 fusion.24
  818.7 0.2 fusion.25
  819.0 45.8 %psum.25 = f32[1024]{0:T(1024)S(1)} all-reduce(f32[1024]{0:T(1024)S(1)} %bitcast.49), channel_id=1, replica_groups=mesh['mem'=32,'space'=16] {'mem'}, use_global_device_ids=true, to_apply=%region_8.0 | all-reduce | flops 1024 | bytes 8192 | tf_op jit(solution)/shard_map/while/body/eval_jaxpr/psum | solution.py:44
  864.8 0.6 broadcast_multiply_fusion
  865.4 0.0 copy-done
  865.4 0.7 multiply_convert_fusion
  866.1 0.0 all-gather.2.cloned.1.call-update
  866.2 70.0 %all-gather.2.cloned.1.call-done = bf16[1024,1024]{1,0:T(8,128)(2,1)} async-done(((bf16[32,1024]{1,0:T(8,128)(2,1)}), bf16[1024,1024]{1,0:T(8,128)(2,1)}) %all-gather.2.cloned.1.call-update) | async-done | bytes 2097168 | tf_op jit(solution)/shard_map/all_gather | solution.py:47
  936.2 2.9 convolution_convert_fusion
  939.0 63.8 %all_to_all.39 = bf16[32,32,512]{2,1,0:T(8,128)(2,1)S(1)} all-to-all(bf16[32,32,512]{2,1,0:T(8,128)(2,1)S(1)} %bitcast.47), channel_id=1, replica_groups=mesh['mem'=32,'space'=16] {'mem'}, dimensions={0} | all-to-all | bytes 2097152 | tf_op jit(solution)/shard_map/all_to_all | solution.py:52
  1002.8 1.1 copy.10
  (42 shorter events, 0.2 us)
Async XLA Ops:
  6.5 179.5 %reduce-scatter.2.cloned.1.call-start = ((), (), s32[]{:S(2)}) async-start(), calls=%async_computation.3 | async-start | bytes 4325376 | tf_op jit(solution)/shard_map/reduce_scatter | solution.py:31
  83.4 1.9 copy-start.1
  83.4 218.0 %all-reduce.3.cloned.1.call-start = ((), (), s32[]{:S(2)}) async-start(), calls=%async_computation.4 | async-start | bytes 262144 | tf_op jit(solution)/shard_map/psum | solution.py:32
  186.0 750.1 %all-gather.2.cloned.1.call-start = ((), (), s32[]{:S(2)}) async-start(), calls=%async_computation.5 | async-start | bytes 2162688 | tf_op jit(solution)/shard_map/all_gather | solution.py:47
  301.4 564.0 %copy-start = (f32[32,1024]{1,0:T(8,128)S(1)}, f32[32,1024]{1,0:T(8,128)}, u32[]{:S(2)}) copy-start(f32[32,1024]{1,0:T(8,128)} %all-reduce.3.cloned.1.call-done) | copy-start | bytes 393220
  402.4 46.0 %copy-start.2 = (f32[32]{0:T(128)}, f32[32]{0:T(128)S(1)}, u32[]{:S(2)}) copy-start(f32[32]{0:T(128)S(1)} %fusion.24) | copy-start | bytes 388 | tf_op jit(solution)/shard_map/while
  448.7 46.0 %copy-start.2 = (f32[32]{0:T(128)}, f32[32]{0:T(128)S(1)}, u32[]{:S(2)}) copy-start(f32[32]{0:T(128)S(1)} %fusion.24) | copy-start | bytes 388 | tf_op jit(solution)/shard_map/while
  494.9 46.0 %copy-start.2 = (f32[32]{0:T(128)}, f32[32]{0:T(128)S(1)}, u32[]{:S(2)}) copy-start(f32[32]{0:T(128)S(1)} %fusion.24) | copy-start | bytes 388 | tf_op jit(solution)/shard_map/while
  541.2 46.0 %copy-start.2 = (f32[32]{0:T(128)}, f32[32]{0:T(128)S(1)}, u32[]{:S(2)}) copy-start(f32[32]{0:T(128)S(1)} %fusion.24) | copy-start | bytes 388 | tf_op jit(solution)/shard_map/while
  587.4 46.0 %copy-start.2 = (f32[32]{0:T(128)}, f32[32]{0:T(128)S(1)}, u32[]{:S(2)}) copy-start(f32[32]{0:T(128)S(1)} %fusion.24) | copy-start | bytes 388 | tf_op jit(solution)/shard_map/while
  633.7 46.0 %copy-start.2 = (f32[32]{0:T(128)}, f32[32]{0:T(128)S(1)}, u32[]{:S(2)}) copy-start(f32[32]{0:T(128)S(1)} %fusion.24) | copy-start | bytes 388 | tf_op jit(solution)/shard_map/while
  680.0 46.0 %copy-start.2 = (f32[32]{0:T(128)}, f32[32]{0:T(128)S(1)}, u32[]{:S(2)}) copy-start(f32[32]{0:T(128)S(1)} %fusion.24) | copy-start | bytes 388 | tf_op jit(solution)/shard_map/while
  726.2 46.0 %copy-start.2 = (f32[32]{0:T(128)}, f32[32]{0:T(128)S(1)}, u32[]{:S(2)}) copy-start(f32[32]{0:T(128)S(1)} %fusion.24) | copy-start | bytes 388 | tf_op jit(solution)/shard_map/while
  772.5 46.0 %copy-start.2 = (f32[32]{0:T(128)}, f32[32]{0:T(128)S(1)}, u32[]{:S(2)}) copy-start(f32[32]{0:T(128)S(1)} %fusion.24) | copy-start | bytes 388 | tf_op jit(solution)/shard_map/while
  818.7 46.0 %copy-start.2 = (f32[32]{0:T(128)}, f32[32]{0:T(128)S(1)}, u32[]{:S(2)}) copy-start(f32[32]{0:T(128)S(1)} %fusion.24) | copy-start | bytes 388 | tf_op jit(solution)/shard_map/while
Sparse Core Ops, SparseCore 0:
  83.5 102.4 reduce-scatter.1
  189.2 112.2 all-reduce.2
  866.3 69.8 all-gather.1
where the time goes:
time: 1010 us
  blocking collectives  690 us (68%)
  waiting for transfers between devices  283 us (28%)
  between operations  14.4 us (1%)
  matrix products  10.1 us (1%)
    psum x10, blocking collectives, column_total(): return lax.psum(values, 'mem')  458 us
    psum x1, waiting for transfers between devices, per_device(): gram_rows = lax.psum(local_rows, 'space')  114 us
    reduce_scatter x1, waiting for transfers between devices, per_device(): lax.psum_scatter(partial_gram, 'mem', scatter_dimension=0, tiled=True)  98.8 us
    all_to_all x1, blocking collectives, per_device(): lax.all_to_all(ensemble, 'mem', split_axis=1, concat_axis=0, tiled=True)  72.3 us
    all_gather x1, waiting for transfers between devices, per_device(): coupling = lax.all_gather(coupling_rows, 'mem', axis=0, tiled=True)  70 us
    all_to_all x1, blocking collectives, per_device(): return lax.all_to_all(mixed, 'mem', split_axis=0, concat_axis=1, tiled=True)  63.8 us
    unnamed x1, blocking collectives  48.6 us
    psum x1, blocking collectives, per_device(): dist_total = lax.psum(jnp.sum(dist), 'mem')  47.1 us
  transfers between devices with their start and end apart: 3, of which 3 were waited for; matrix products, arithmetic and copies ran while one was open for 0% of the time, Pallas kernels for 0%

commit v1 on v0

--- a/solution.py
+++ b/solution.py
@@ -44,7 +44,9 @@
         return lax.psum(values, "mem")
 
     coupling_rows = coupling_from(kernel, weights_rows, column_total)
-    coupling = lax.all_gather(coupling_rows, "mem", axis=0, tiled=True)
+    coupling = jnp.concatenate(
+        lax.all_to_all(jnp.stack(lax.psum(1, "mem") * [coupling_rows], axis=0), "mem", 0, 0), axis=0
+    )
     mixed = lax.dot_general(
         coupling, relaid, (((0,), (0,)), ((), ())), preferred_element_type=jnp.float32
     )

time: 1010 us -> 1050 us (1.040)
  blocking collectives: 690 us -> 797 us
  waiting for transfers between devices: 283 us -> 213 us
    all_to_all x0 -> x1, blocking collectives: none -> 112 us  [per_device(): lax.all_to_all(jnp.stack(lax.psum(1, 'mem') * [coupling_rows], axis=0), '...]
    all_gather x1 -> x0, waiting for transfers between devices: 70 us -> none  [per_device(): coupling = lax.all_gather(coupling_rows, 'mem', axis=0, tiled=True)]
  transfers between devices with their start and end apart: 3 -> 2, of which waited for: 3 -> 2; matrix products, arithmetic and copies ran while one was open for 0% -> 0% of each run, Pallas kernels for 0% -> 0%
where the time goes in v1:
time: 1050 us
  blocking collectives  797 us (76%)
  waiting for transfers between devices  213 us (20%)
  between operations  14.7 us (1%)
    psum x10, blocking collectives, column_total(): return lax.psum(values, 'mem')  458 us
    psum x1, waiting for transfers between devices, per_device(): gram_rows = lax.psum(local_rows, 'space')  114 us
    all_to_all x1, blocking collectives, per_device(): lax.all_to_all(jnp.stack(lax.psum(1, 'mem') * [coupling_rows], axis=0), '...  112 us
    reduce_scatter x1, waiting for transfers between devices, per_device(): lax.psum_scatter(partial_gram, 'mem', scatter_dimension=0, tiled=True)  98.8 us
    all_to_all x1, blocking collectives, per_device(): lax.all_to_all(ensemble, 'mem', split_axis=1, concat_axis=0, tiled=True)  72.3 us
    all_to_all x1, blocking collectives, per_device(): return lax.all_to_all(mixed, 'mem', split_axis=0, concat_axis=1, tiled=True)  59 us
    unnamed x1, blocking collectives  48.6 us
    psum x1, blocking collectives, per_device(): dist_total = lax.psum(jnp.sum(dist), 'mem')  47.1 us
  transfers between devices with their start and end apart: 2, of which 2 were waited for; matrix products, arithmetic and copies ran while one was open for 0% of the time, Pallas kernels for 0%

profile of v1, /device:TPU:1, one launch (start us, length us, event | category | flops | bytes accessed | tf_op | source)
XLA Modules:
  0.0 1045.6 jit_solution(998897535589940340)
XLA Ops:
  6.5 0.0 reduce-scatter.2.cloned.1.call-start
  6.5 1.4 copy.9
  7.9 72.3 %all_to_all.43 = bf16[32,32,512]{2,0,1:T(8,128)(2,1)S(1)} all-to-all(bf16[32,32,512]{2,0,1:T(8,128)(2,1)S(1)} %bitcast.46), channel_id=1, replica_groups=mesh['mem'=32,'space'=16] {'mem'}, dimensions={1} | all-to-all | bytes 2097152 | tf_op jit(solution)/shard_map/all_to_all | solution.py:26
  80.2 3.2 fusion.7
  83.4 0.0 reduce-scatter.2.cloned.1.call-update
  83.4 0.0 all-reduce.3.cloned.1.call-start
  83.5 1.3 dynamic-slice
  85.3 0.0 copy-done.1
  85.3 0.6 reduce_max.9
  85.9 1.2 fusion.6
  87.2 98.8 %reduce-scatter.2.cloned.1.call-done = f32[32,1024]{1,0:T(8,128)} async-done(((f32[1024,1024]{1,0:T(8,128)}), f32[32,1024]{1,0:T(8,128)}) %reduce-scatter.2.cloned.1.call-update) | async-done | bytes 131088 | tf_op jit(solution)/shard_map/reduce_scatter | solution.py:31
  186.0 0.0 all-reduce.3.cloned.1.call-update
  186.0 1.2 fusion.5
  187.3 0.1 dynamic_slice.6
  187.3 114.1 %all-reduce.3.cloned.1.call-done = f32[32,1024]{1,0:T(8,128)} async-done(((f32[32,1024]{1,0:T(8,128)}), f32[32,1024]{1,0:T(8,128)}) %all-reduce.3.cloned.1.call-update) | async-done | bytes 131088 | tf_op jit(solution)/shard_map/psum | solution.py:32
  301.4 1.0 select_reduce_fusion
  302.4 0.2 dynamic-update-slice
  302.7 48.6 %all-reduce = f32[1024]{0:T(1024)S(1)} all-reduce(f32[1024]{0:T(1024)S(1)} %dynamic-update-slice), channel_id=1, replica_groups=mesh['mem'=32,'space'=16] {'mem'}, use_global_device_ids=true, to_apply=%add | all-reduce | flops 1024 | bytes 8192
  351.2 1.7 fusion.4
  352.9 0.5 copy.13
  353.4 47.1 %psum.22 = f32[]{:T(128)} all-reduce(f32[]{:T(128)} %fusion.4), channel_id=1, replica_groups=mesh['mem'=32,'space'=16] {'mem'}, use_global_device_ids=true, to_apply=%region_6.0 | all-reduce | flops 1 | bytes 8 | tf_op jit(solution)/shard_map/psum | solution.py:38
  401.2 1.0 divide_exponential_fusion
  402.2 462.6 %while.13 = (s32[]{:T(128)}, f32[32]{0:T(128)}, f32[1024]{0:T(1024)S(1)}, f32[32,1024]{1,0:T(8,128)S(1)}, f32[32]{0:T(128)S(1)}, /*index=5*/s32[]{:T(128)}, s32[]{:T(128)}) while((s32[]{:T(128)}, f32[32]{0:T(128)}, f32[1024]{0:T(1024)S(1)}, f32[32,1024]{1,0:T(8,128)S(1)}, f32[32]{0:T(128)S(1)}, /*index=5*/s32[]{:T(128)}, ...), condition=%wide.region_9.0_spmd.clone, body=%wide.region_7.0_spmd.clone.sunk | while | flops 789539 | bytes 295923 | solution.py:19
  402.2 0.2 fusion.24
  402.4 0.2 fusion.25
  402.6 45.8 %psum.25 = f32[1024]{0:T(1024)S(1)} all-reduce(f32[1024]{0:T(1024)S(1)} %bitcast.51), channel_id=1, replica_groups=mesh['mem'=32,'space'=16] {'mem'}, use_global_device_ids=true, to_apply=%region_8.0 | all-reduce | flops 1024 | bytes 8192 | tf_op jit(solution)/shard_map/while/body/eval_jaxpr/psum | solution.py:44
  448.4 0.0 copy-done.2
  448.5 0.2 fusion.24
  448.7 0.2 fusion.25
  448.9 45.8 %psum.25 = f32[1024]{0:T(1024)S(1)} all-reduce(f32[1024]{0:T(1024)S(1)} %bitcast.51), channel_id=1, replica_groups=mesh['mem'=32,'space'=16] {'mem'}, use_global_device_ids=true, to_apply=%region_8.0 | all-reduce | flops 1024 | bytes 8192 | tf_op jit(solution)/shard_map/while/body/eval_jaxpr/psum | solution.py:44
  494.7 0.2 fusion.24
  494.9 0.2 fusion.25
  495.2 45.8 %psum.25 = f32[1024]{0:T(1024)S(1)} all-reduce(f32[1024]{0:T(1024)S(1)} %bitcast.51), channel_id=1, replica_groups=mesh['mem'=32,'space'=16] {'mem'}, use_global_device_ids=true, to_apply=%region_8.0 | all-reduce | flops 1024 | bytes 8192 | tf_op jit(solution)/shard_map/while/body/eval_jaxpr/psum | solution.py:44
  541.0 0.0 copy-done.2
  541.0 0.2 fusion.24
  541.2 0.2 fusion.25
  541.4 45.8 %psum.25 = f32[1024]{0:T(1024)S(1)} all-reduce(f32[1024]{0:T(1024)S(1)} %bitcast.51), channel_id=1, replica_groups=mesh['mem'=32,'space'=16] {'mem'}, use_global_device_ids=true, to_apply=%region_8.0 | all-reduce | flops 1024 | bytes 8192 | tf_op jit(solution)/shard_map/while/body/eval_jaxpr/psum | solution.py:44
  587.3 0.2 fusion.24
  587.4 0.2 fusion.25
  587.7 45.8 %psum.25 = f32[1024]{0:T(1024)S(1)} all-reduce(f32[1024]{0:T(1024)S(1)} %bitcast.51), channel_id=1, replica_groups=mesh['mem'=32,'space'=16] {'mem'}, use_global_device_ids=true, to_apply=%region_8.0 | all-reduce | flops 1024 | bytes 8192 | tf_op jit(solution)/shard_map/while/body/eval_jaxpr/psum | solution.py:44
  633.5 0.2 fusion.24
  633.7 0.2 fusion.25
  633.9 45.8 %psum.25 = f32[1024]{0:T(1024)S(1)} all-reduce(f32[1024]{0:T(1024)S(1)} %bitcast.51), channel_id=1, replica_groups=mesh['mem'=32,'space'=16] {'mem'}, use_global_device_ids=true, to_apply=%region_8.0 | all-reduce | flops 1024 | bytes 8192 | tf_op jit(solution)/shard_map/while/body/eval_jaxpr/psum | solution.py:44
  679.8 0.2 fusion.24
  680.0 0.2 fusion.25
  680.2 45.8 %psum.25 = f32[1024]{0:T(1024)S(1)} all-reduce(f32[1024]{0:T(1024)S(1)} %bitcast.51), channel_id=1, replica_groups=mesh['mem'=32,'space'=16] {'mem'}, use_global_device_ids=true, to_apply=%region_8.0 | all-reduce | flops 1024 | bytes 8192 | tf_op jit(solution)/shard_map/while/body/eval_jaxpr/psum | solution.py:44
  726.0 0.0 copy-done.2
  726.0 0.2 fusion.24
  726.2 0.2 fusion.25
  726.5 45.8 %psum.25 = f32[1024]{0:T(1024)S(1)} all-reduce(f32[1024]{0:T(1024)S(1)} %bitcast.51), channel_id=1, replica_groups=mesh['mem'=32,'space'=16] {'mem'}, use_global_device_ids=true, to_apply=%region_8.0 | all-reduce | flops 1024 | bytes 8192 | tf_op jit(solution)/shard_map/while/body/eval_jaxpr/psum | solution.py:44
  772.3 0.2 fusion.24
  772.5 0.2 fusion.25
  772.7 45.8 %psum.25 = f32[1024]{0:T(1024)S(1)} all-reduce(f32[1024]{0:T(1024)S(1)} %bitcast.51), channel_id=1, replica_groups=mesh['mem'=32,'space'=16] {'mem'}, use_global_device_ids=true, to_apply=%region_8.0 | all-reduce | flops 1024 | bytes 8192 | tf_op jit(solution)/shard_map/while/body/eval_jaxpr/psum | solution.py:44
  818.6 0.2 fusion.24
  818.7 0.2 fusion.25
  819.0 45.8 %psum.25 = f32[1024]{0:T(1024)S(1)} all-reduce(f32[1024]{0:T(1024)S(1)} %bitcast.51), channel_id=1, replica_groups=mesh['mem'=32,'space'=16] {'mem'}, use_global_device_ids=true, to_apply=%region_8.0 | all-reduce | flops 1024 | bytes 8192 | tf_op jit(solution)/shard_map/while/body/eval_jaxpr/psum | solution.py:44
  864.8 0.0 copy-done.2
  864.8 0.6 broadcast_multiply_fusion
  865.4 0.1 multiply_convert_fusion
  865.5 0.2 stack.2
  865.8 111.6 %all_to_all.44 = bf16[32,32,1024]{2,1,0:T(8,128)(2,1)S(1)} all-to-all(bf16[32,32,1024]{2,1,0:T(8,128)(2,1)S(1)} %stack.2), channel_id=1, replica_groups=mesh['mem'=32,'space'=16] {'mem'}, dimensions={0} | all-to-all | bytes 4194304 | tf_op jit(solution)/shard_map/all_to_all | solution.py:48
  977.4 1.3 bitcast_convert_fusion
  978.7 59.0 %all_to_all.45 = bf16[32,32,512]{2,1,0:T(8,128)(2,1)S(1)} all-to-all(bf16[32,32,512]{2,1,0:T(8,128)(2,1)S(1)} %bitcast.49), channel_id=1, replica_groups=mesh['mem'=32,'space'=16] {'mem'}, dimensions={0} | all-to-all | bytes 2097152 | tf_op jit(solution)/shard_map/all_to_all | solution.py:54
  1037.7 1.1 copy.7
  (41 shorter events, 0.2 us)
Async XLA Ops:
  6.5 179.5 %reduce-scatter.2.cloned.1.call-start = ((), (), s32[]{:S(2)}) async-start(), calls=%async_computation.4 | async-start | bytes 4325376 | tf_op jit(solution)/shard_map/reduce_scatter | solution.py:31
  83.4 1.9 copy-start.1
  83.4 218.0 %all-reduce.3.cloned.1.call-start = ((), (), s32[]{:S(2)}) async-start(), calls=%async_computation.5 | async-start | bytes 262144 | tf_op jit(solution)/shard_map/psum | solution.py:32
  301.4 564.0 %copy-start = (f32[32,1024]{1,0:T(8,128)S(1)}, f32[32,1024]{1,0:T(8,128)}, u32[]{:S(2)}) copy-start(f32[32,1024]{1,0:T(8,128)} %all-reduce.3.cloned.1.call-done) | copy-start | bytes 393220
  402.4 46.0 %copy-start.2 = (f32[32]{0:T(128)}, f32[32]{0:T(128)S(1)}, u32[]{:S(2)}) copy-start(f32[32]{0:T(128)S(1)} %fusion.24) | copy-start | bytes 388 | tf_op jit(solution)/shard_map/while
  448.7 46.0 %copy-start.2 = (f32[32]{0:T(128)}, f32[32]{0:T(128)S(1)}, u32[]{:S(2)}) copy-start(f32[32]{0:T(128)S(1)} %fusion.24) | copy-start | bytes 388 | tf_op jit(solution)/shard_map/while
  494.9 46.0 %copy-start.2 = (f32[32]{0:T(128)}, f32[32]{0:T(128)S(1)}, u32[]{:S(2)}) copy-start(f32[32]{0:T(128)S(1)} %fusion.24) | copy-start | bytes 388 | tf_op jit(solution)/shard_map/while
  541.2 46.0 %copy-start.2 = (f32[32]{0:T(128)}, f32[32]{0:T(128)S(1)}, u32[]{:S(2)}) copy-start(f32[32]{0:T(128)S(1)} %fusion.24) | copy-start | bytes 388 | tf_op jit(solution)/shard_map/while
  587.4 46.0 %copy-start.2 = (f32[32]{0:T(128)}, f32[32]{0:T(128)S(1)}, u32[]{:S(2)}) copy-start(f32[32]{0:T(128)S(1)} %fusion.24) | copy-start | bytes 388 | tf_op jit(solution)/shard_map/while
  633.7 46.0 %copy-start.2 = (f32[32]{0:T(128)}, f32[32]{0:T(128)S(1)}, u32[]{:S(2)}) copy-start(f32[32]{0:T(128)S(1)} %fusion.24) | copy-start | bytes 388 | tf_op jit(solution)/shard_map/while
  680.0 46.0 %copy-start.2 = (f32[32]{0:T(128)}, f32[32]{0:T(128)S(1)}, u32[]{:S(2)}) copy-start(f32[32]{0:T(128)S(1)} %fusion.24) | copy-start | bytes 388 | tf_op jit(solution)/shard_map/while
  726.2 46.0 %copy-start.2 = (f32[32]{0:T(128)}, f32[32]{0:T(128)S(1)}, u32[]{:S(2)}) copy-start(f32[32]{0:T(128)S(1)} %fusion.24) | copy-start | bytes 388 | tf_op jit(solution)/shard_map/while
  772.5 46.0 %copy-start.2 = (f32[32]{0:T(128)}, f32[32]{0:T(128)S(1)}, u32[]{:S(2)}) copy-start(f32[32]{0:T(128)S(1)} %fusion.24) | copy-start | bytes 388 | tf_op jit(solution)/shard_map/while
  818.7 46.0 %copy-start.2 = (f32[32]{0:T(128)}, f32[32]{0:T(128)S(1)}, u32[]{:S(2)}) copy-start(f32[32]{0:T(128)S(1)} %fusion.24) | copy-start | bytes 388 | tf_op jit(solution)/shard_map/while
Sparse Core Ops, SparseCore 0:
  83.5 102.4 reduce-scatter.1
  189.2 112.2 all-reduce.2
